TPU v7x, 256 devices: a whole 4x4x8 slice. The times are simulated.
256 devices in a mesh: expert: 64 (over z, x, core), tensor: 4 (over y).
Axes of the slice: x: 4, y: 4, z: 8, core: 2. Of those that a mesh axis runs over, the one named last changes fastest.
Arguments:
- tokens: bfloat16 [2048, 4096], P('expert', 'tensor'), may hold values from -6 to 6
- cotangent: bfloat16 [2048, 4096], P('expert', 'tensor'), may hold values from -6 to 6
- routing: int32 [2048, 8], P('expert'), may hold values from 0 to 63, as said below
- gates: float32 [2048, 8], P('expert'), may hold values from 0.1 to 0.4
- w_in: bfloat16 [64, 4096, 1536], P('expert', None, 'tensor'), may hold values from -0.09375 to 0.09375
- w_out: bfloat16 [64, 1536, 4096], P('expert', 'tensor'), may hold values from -0.15625 to 0.15625
Outputs:
- mixed: bfloat16 [2048, 4096], P('expert', 'tensor')
- d_tokens: bfloat16 [2048, 4096], P('expert', 'tensor')
- d_w_in: bfloat16 [64, 4096, 1536], P('expert', None, 'tensor')
- d_w_out: bfloat16 [64, 1536, 4096], P('expert', 'tensor')
Inputs may be any that keep to these rules, and one draw needn't show every extreme that they name: `routing`: each row names 8 different experts. In each aligned block of 32 rows (the tokens of one index of the expert axis) no expert is named by more than 8 rows, and one expert is named by exactly 8 rows of every block.
All inputs are finite; a program needn't handle non-finite values.
Results may differ from a plain program's by a relative error of at most 0.0058.
Values may be sent and summed in bfloat16 or wider, within the bound.
A program may use at most 128 MiB of HBM per device.

v0:
```python
import jax
import jax.numpy as jnp
from jax import lax
from jax.sharding import PartitionSpec as P


def shards(tokens, cotangent, routing, gates, w_in, w_out):
    devices = lax.axis_size("expert")
    local_experts = w_in.shape[0]
    experts = devices * local_experts
    tok_rows = routing.shape[0]
    capacity = tok_rows // 4
    buffer_rows = experts * capacity
    highest = lax.Precision.HIGHEST
    matches = (routing[:, :, None] == jnp.arange(experts, dtype=jnp.int32)[None, None, :]).astype(
        jnp.int32
    )
    per_token = jnp.sum(matches, axis=1)
    earlier = jnp.cumsum(per_token, axis=0) - per_token
    destination = routing * capacity + jnp.take_along_axis(earlier, routing, axis=1)
    placed = (
        destination[:, :, None] == jnp.arange(buffer_rows, dtype=jnp.int32)[None, None, :]
    ).astype(jnp.float32)
    membership = jnp.sum(placed, axis=1)
    weighting = jnp.sum(placed * gates[:, :, None], axis=1)
    quarter = tokens.shape[1]
    rows = jnp.einsum(
        "tr,td->rd", membership.astype(jnp.bfloat16), tokens, preferred_element_type=jnp.float32
    ).astype(jnp.bfloat16)
    scaled = jnp.einsum(
        "tr,td->rd", weighting, cotangent.astype(jnp.float32), precision=highest
    ).astype(jnp.bfloat16)
    send = jnp.concatenate(
        [
            rows.reshape(devices, local_experts, capacity, quarter),
            scaled.reshape(devices, local_experts, capacity, quarter),
        ],
        axis=2,
    )
    arrived = lax.all_to_all(send, "expert", split_axis=0, concat_axis=0, tiled=True)
    whole = lax.all_gather(arrived, "tensor", axis=3, tiled=True)
    expert_rows = whole[:, :, :capacity]
    expert_scaled = whole[:, :, capacity:]
    preact = jnp.einsum("nesd,edh->nesh", expert_rows, w_in, preferred_element_type=jnp.float32)
    sigmoid_val = jax.nn.sigmoid(preact)
    hidden = (preact * sigmoid_val).astype(jnp.bfloat16)
    out_part = jnp.einsum("nesh,ehd->nesd", hidden, w_out, preferred_element_type=jnp.float32)
    grad_hidden = jnp.einsum(
        "nesd,ehd->nesh", expert_scaled, w_out, preferred_element_type=jnp.float32
    )
    grad_preact = (grad_hidden * sigmoid_val * (1.0 + preact * (1.0 - sigmoid_val))).astype(
        jnp.bfloat16
    )
    d_w_out = jnp.einsum(
        "nesh,nesd->ehd", hidden, expert_scaled, preferred_element_type=jnp.float32
    ).astype(jnp.bfloat16)
    d_w_in = jnp.einsum(
        "nesd,nesh->edh", expert_rows, grad_preact, preferred_element_type=jnp.float32
    ).astype(jnp.bfloat16)
    grad_part = jnp.einsum("nesh,edh->nesd", grad_preact, w_in, preferred_element_type=jnp.float32)
    parts = jnp.concatenate([out_part.astype(jnp.bfloat16), grad_part.astype(jnp.bfloat16)], axis=2)
    sums = lax.psum_scatter(parts, "tensor", scatter_dimension=3, tiled=True)
    back = lax.all_to_all(sums, "expert", split_axis=0, concat_axis=0, tiled=True)
    back_out = back[:, :, :capacity].reshape(buffer_rows, quarter).astype(jnp.float32)
    back_grad = back[:, :, capacity:].reshape(buffer_rows, quarter).astype(jnp.float32)
    mixed = jnp.einsum("tr,rd->td", weighting, back_out, precision=highest).astype(jnp.bfloat16)
    d_tokens = jnp.einsum("tr,rd->td", membership, back_grad, precision=highest).astype(
        jnp.bfloat16
    )
    return (mixed, d_tokens, d_w_in, d_w_out)


def solution(mesh):
    placed = (
        P("expert", "tensor"),
        P("expert", "tensor"),
        P("expert", None),
        P("expert", None),
        P("expert", None, "tensor"),
        P("expert", "tensor", None),
    )
    return jax.shard_map(
        shards,
        mesh=mesh,
        in_specs=placed,
        out_specs=(
            P("expert", "tensor"),
            P("expert", "tensor"),
            P("expert", None, "tensor"),
            P("expert", "tensor", None),
        ),
        check_vma=False,
    )
```

profile of v0, /device:TPU:2, one launch (start us, length us, event | category | flops | bytes accessed | tf_op | source)
XLA Modules:
  0.0 343.1 jit_solution(5815221899172722763)
XLA Ops:
  7.2 0.0 copy-start
  7.2 0.0 all-gather.2.cloned.1.call-start
  7.2 0.8 bitcast_or_fusion
  8.1 0.8 copy.47
  8.9 0.1 copy.48
  9.0 0.1 reshape.77
  9.1 0.8 copy.51
  9.8 0.1 convert_reduce_fusion.1
  9.9 0.1 reduce_window_sum.11
  10.0 0.0 copy-start.3
  10.0 0.0 copy-start.1
  10.0 0.0 copy-start.2
  10.0 1.9 gather_fusion
  12.0 0.1 reshape.80
  12.1 0.1 copy.49
  12.1 0.0 copy-done.3
  12.2 0.1 copy.50
  12.2 0.4 convert_reduce_fusion
  12.6 0.0 copy-done.1
  12.6 0.5 fusion.10
  13.1 0.0 copy-done.2
  13.1 1.0 fusion.11
  14.1 0.2 pad_maximum_fusion.1
  14.4 63.2 %all_to_all.10 = bf16[64,1,16,1024]{3,2,1,0:T(8,128)(2,1)} all-to-all(bf16[64,1,16,1024]{3,2,1,0:T(8,128)(2,1)S(1)} %pad_maximum_fusion.1), channel_id=1, replica_groups=mesh['expert'=64,'tensor'=4] {'expert'}, dimensions={0} | all-to-all | bytes 4194304 | tf_op jit(solution)/shard_map/all_to_all | solution.py:40
  77.6 0.0 all-gather.2.cloned.1.call-update
  77.6 0.2 reduce-scatter.2.cloned.1.call-start
  77.8 82.0 %all-gather.2.cloned.1.call-done = bf16[64,1,16,4096]{3,2,0,1:T(8,128)(2,1)} async-done(((bf16[64,1,16,1024]{3,2,0,1:T(8,128)(2,1)}), bf16[64,1,16,4096]{3,2,0,1:T(8,128)(2,1)}) %all-gather.2.cloned.1.call-update) | async-done | bytes 8388624 | tf_op jit(solution)/shard_map/all_gather | solution.py:41
  159.8 5.5 %fusion.18 = f32[64,1,8,384]{3,2,0,1:T(8,128)S(1)} fusion(bf16[1,4096,384]{2,1,0:T(8,128)(2,1)} %param.10, bf16[64,1,16,4096]{3,2,0,1:T(8,128)(2,1)} %all-gather.2.cloned.1.call-done), kind=kOutput, calls=%fused_computation.25 | convolution fusion | flops 1610612736 | bytes 8126464 | tf_op jit(solution)/shard_map/nesd,edh->nesh/dot_general | solution.py:44
  165.3 0.0 copy-done
  165.3 0.0 copy-start.7
  165.3 0.0 copy-start.4
  165.3 4.3 %fusion = bf16[64,1,8,4096]{3,2,0,1:T(8,128)(2,1)} fusion(bf16[1,384,4096]{2,1,0:T(8,128)(2,1)S(1)} %copy-done, f32[64,1,8,384]{3,2,0,1:T(8,128)S(1)} %fusion.18), kind=kOutput, calls=%fused_computation.6 | convolution fusion | flops 1613692928 | bytes 8126464 | tf_op jit(solution)/shard_map/nesh,ehd->nesd/dot_general | solution.py:47
  169.6 0.0 copy-done.7
  169.6 0.1 copy-done.4
  169.8 2.4 fusion.27
  172.2 0.0 copy-start.6
  172.2 0.8 copy-done.6
  173.0 0.0 copy-done.5
  173.0 4.3 %fusion.1 = bf16[64,1,8,4096]{3,2,0,1:T(8,128)(2,1)} fusion(bf16[64,8,384]{2,1,0:T(8,128)(2,1)S(1)} %fusion.27, bf16[1,4096,384]{2,1,0:T(8,128)(2,1)S(1)} %copy-done.5), kind=kOutput, calls=%fused_computation.7 | convolution fusion | flops 1612709888 | bytes 7733248 | tf_op jit(solution)/shard_map/nesh,edh->nesd/dot_general | solution.py:60
  177.4 7.8 %pad_maximum_fusion = bf16[64,1,16,4096]{3,2,0,1:T(8,128)(2,1)} fusion(bf16[64,1,8,4096]{3,2,0,1:T(8,128)(2,1)} %fusion.1, bf16[64,1,8,4096]{3,2,0,1:T(8,128)(2,1)} %fusion), kind=kLoop, calls=%fused_computation.1 | loop fusion | flops 16777216 | bytes 16777216 | tf_op jit(solution)/shard_map/concatenate | solution.py:61
  185.2 0.0 reduce-scatter.2.cloned.1.call-update
  185.2 6.0 %fusion.3 = bf16[1,384,4096]{2,1,0:T(8,128)(2,1)} fusion(bf16[64,1,16,4096]{3,2,0,1:T(8,128)(2,1)} %all-gather.2.cloned.1.call-done, f32[64,1,8,384]{3,2,0,1:T(8,128)} %copy-done.7), kind=kOutput, calls=%fused_computation.9 | convolution fusion | flops 1613168640 | bytes 8126464 | tf_op jit(solution)/shard_map/nesh,nesd->ehd/dot_general | solution.py:54
  191.2 78.3 %reduce-scatter.2.cloned.1.call-done = bf16[64,1,16,1024]{3,2,0,1:T(8,128)(2,1)} async-done(((bf16[64,1,16,4096]{3,2,0,1:T(8,128)(2,1)}), bf16[64,1,16,1024]{3,2,0,1:T(8,128)(2,1)}) %reduce-scatter.2.cloned.1.call-update) | async-done | bytes 2097168 | tf_op jit(solution)/shard_map/reduce_scatter | solution.py:62
  269.4 10.7 %all-to-all-start.1 = ((bf16[64,1,16,1024]{3,2,1,0:T(8,128)(2,1)}), bf16[64,1,16,1024]{3,2,1,0:T(8,128)(2,1)}, u32[]{:S(2)}, u32[]{:S(2)}) async-start(bf16[64,1,16,1024]{3,2,1,0:T(8,128)(2,1)} %bitcast.123), calls=%async_computation.2 | async-start | bytes 4194304 | tf_op jit(solution)/shard_map/all_to_all | solution.py:63
  280.2 6.3 %fusion.2 = bf16[1,4096,384]{2,1,0:T(8,128)(2,1)} fusion(bf16[64,8,384]{2,1,0:T(8,128)(2,1)} %copy-done.6, bf16[64,1,16,4096]{3,2,0,1:T(8,128)(2,1)} %all-gather.2.cloned.1.call-done), kind=kOutput, calls=%fused_computation.8 | convolution fusion | flops 1612185600 | bytes 7733248 | tf_op jit(solution)/shard_map/nesd,nesh->edh/dot_general | solution.py:57
  286.5 44.9 %all-to-all-done.1 = bf16[64,1,16,1024]{3,2,1,0:T(8,128)(2,1)} async-done(((bf16[64,1,16,1024]{3,2,1,0:T(8,128)(2,1)}), bf16[64,1,16,1024]{3,2,1,0:T(8,128)(2,1)}, u32[]{:S(2)}, u32[]{:S(2)}) %all-to-all-start.1) | async-done | bytes 2097184 | tf_op jit(solution)/shard_map/all_to_all | solution.py:63
  331.3 2.5 convolution_convert_fusion.4
  333.8 2.5 convolution_convert_fusion.5
  (3 shorter events, 0.0 us)
Async XLA Ops:
  7.2 158.1 %copy-start = (bf16[1,384,4096]{2,1,0:T(8,128)(2,1)S(1)}, bf16[1,384,4096]{2,1,0:T(8,128)(2,1)}, u32[]{:S(2)}) copy-start(bf16[1,384,4096]{2,1,0:T(8,128)(2,1)} %param.11) | copy-start | bytes 9437188
  7.2 152.6 %all-gather.2.cloned.1.call-start = ((), (), s32[]{:S(2)}) async-start(), calls=%async_computation.3 | async-start | bytes 10485760 | tf_op jit(solution)/shard_map/all_gather | solution.py:41
  10.0 2.1 copy-start.3
  10.0 2.6 copy-start.1
  10.0 3.1 copy-start.2
  77.6 191.8 %reduce-scatter.2.cloned.1.call-start = ((), (), s32[]{:S(2)}) async-start(), calls=%async_computation.4 | async-start | bytes 10485760 | tf_op jit(solution)/shard_map/reduce_scatter | solution.py:62
  165.3 4.3 %copy-start.7 = (f32[64,1,8,384]{3,2,0,1:T(8,128)}, f32[64,1,8,384]{3,2,0,1:T(8,128)S(1)}, u32[]{:S(2)}) copy-start(f32[64,1,8,384]{3,2,0,1:T(8,128)S(1)} %fusion.18) | copy-start | bytes 2359300
  165.3 4.4 %copy-start.4 = (bf16[64,1,16,4096]{3,2,0,1:T(8,128)(2,1)S(1)}, bf16[64,1,16,4096]{3,2,0,1:T(8,128)(2,1)}, u32[]{:S(2)}) copy-start(bf16[64,1,16,4096]{3,2,0,1:T(8,128)(2,1)} %all-gather.2.cloned.1.call-done) | copy-start | bytes 25165828
  169.7 3.3 copy-start.5
  172.2 0.8 copy-start.6
  269.4 61.9 %all-to-all-start.1 = ((bf16[64,1,16,1024]{3,2,1,0:T(8,128)(2,1)}), bf16[64,1,16,1024]{3,2,1,0:T(8,128)(2,1)}, u32[]{:S(2)}, u32[]{:S(2)}) async-start(bf16[64,1,16,1024]{3,2,1,0:T(8,128)(2,1)} %bitcast.123), calls=%async_computation.2 | async-start | bytes 4194304 | tf_op jit(solution)/shard_map/all_to_all | solution.py:63
Sparse Core Ops, SparseCore 0:
  77.7 82.0 all-gather.1
  185.3 84.0 reduce-scatter.1
where the time goes:
time: 343 us
  waiting for transfers between devices  205 us (60%)
  blocking collectives  63.2 us (18%)
  matrix products  35.2 us (10%)
  between operations  14.2 us (4%)
  starting transfers between devices  11 us (3%)
  other arithmetic  9.46 us (3%)
  local copies, waits for them, and re-layouts  4.91 us (1%)
    all_gather x1, waiting for transfers between devices, shards(): whole = lax.all_gather(arrived, 'tensor', axis=3, tiled=True)  82 us
    reduce_scatter x1, waiting for transfers between devices, shards(): sums = lax.psum_scatter(parts, 'tensor', scatter_dimension=3, tiled=True)  78.3 us
    all_to_all x1, blocking collectives, shards(): lax.all_to_all(send, 'expert', split_axis=0, concat_axis=0, tiled=True)  63.2 us
    all_to_all x1, waiting for transfers between devices, shards(): lax.all_to_all(sums, 'expert', split_axis=0, concat_axis=0, tiled=True)  44.9 us
    all_to_all x1, starting transfers between devices, shards(): lax.all_to_all(sums, 'expert', split_axis=0, concat_axis=0, tiled=True)  10.7 us
    concatenate x1, other arithmetic, shards(): jnp.concatenate([out_part.astype(jnp.bfloat16), grad_part.astype(jnp.bflo...  7.8 us
  transfers between devices with their start and end apart: 3, of which 3 were waited for; matrix products, arithmetic and copies ran while one was open for 4% of the time, Pallas kernels for 0%

commit v1 on v0

--- a/solution.py
+++ b/solution.py
@@ -38,7 +38,9 @@
         axis=2,
     )
     arrived = lax.all_to_all(send, "expert", split_axis=0, concat_axis=0, tiled=True)
-    whole = lax.all_gather(arrived, "tensor", axis=3, tiled=True)
+    whole = jnp.concatenate(
+        lax.all_to_all(jnp.stack([arrived] * lax.axis_size("tensor")), "tensor", 0, 0), axis=3
+    )
     expert_rows = whole[:, :, :capacity]
     expert_scaled = whole[:, :, capacity:]
     preact = jnp.einsum("nesd,edh->nesh", expert_rows, w_in, preferred_element_type=jnp.float32)

time: 343 us -> 360 us (1.050)
  blocking collectives: 63.2 us -> 160 us
  waiting for transfers between devices: 205 us -> 118 us
  local copies, waits for them, and re-layouts: 4.91 us -> 13.2 us
    all_to_all x0 -> x1, blocking collectives: none -> 96.7 us  [shards(): lax.all_to_all(jnp.stack([arrived] * lax.axis_size('tensor')), 'tensor',...]
    all_gather x1 -> x0, waiting for transfers between devices: 82 us -> none  [shards(): whole = lax.all_gather(arrived, 'tensor', axis=3, tiled=True)]
    reshape x0 -> x1, local copies, waits for them, and re-layouts: none -> 8.18 us  [shards(): jnp.concatenate(lax.all_to_all(jnp.stack([arrived] * lax.axis_size('tenso...]
    reduce_scatter x1, waiting for transfers between devices: 78.3 us -> 73 us  [shards(): sums = lax.psum_scatter(parts, 'tensor', scatter_dimension=3, tiled=True)]
  transfers between devices with their start and end apart: 3 -> 2, of which waited for: 3 -> 2; matrix products, arithmetic and copies ran while one was open for 4% -> 3% of each run, Pallas kernels for 0% -> 0%
where the time goes in v1:
time: 360 us
  blocking collectives  160 us (44%)
  waiting for transfers between devices  118 us (33%)
  matrix products  34.4 us (10%)
  between operations  14.2 us (4%)
  local copies, waits for them, and re-layouts  13.2 us (4%)
  starting transfers between devices  11 us (3%)
  other arithmetic  9.44 us (3%)
    all_to_all x1, blocking collectives, shards(): lax.all_to_all(jnp.stack([arrived] * lax.axis_size('tensor')), 'tensor',...  96.7 us
    reduce_scatter x1, waiting for transfers between devices, shards(): sums = lax.psum_scatter(parts, 'tensor', scatter_dimension=3, tiled=True)  73 us
    all_to_all x1, blocking collectives, shards(): lax.all_to_all(send, 'expert', split_axis=0, concat_axis=0, tiled=True)  63.1 us
    all_to_all x1, waiting for transfers between devices, shards(): lax.all_to_all(sums, 'expert', split_axis=0, concat_axis=0, tiled=True)  44.9 us
    all_to_all x1, starting transfers between devices, shards(): lax.all_to_all(sums, 'expert', split_axis=0, concat_axis=0, tiled=True)  10.9 us
    reshape x1, local copies, waits for them, and re-layouts, shards(): jnp.concatenate(lax.all_to_all(jnp.stack([arrived] * lax.axis_size('tenso...  8.18 us
    concatenate x1, other arithmetic, shards(): jnp.concatenate([out_part.astype(jnp.bfloat16), grad_part.astype(jnp.bflo...  7.78 us
  transfers between devices with their start and end apart: 2, of which 2 were waited for; matrix products, arithmetic and copies ran while one was open for 3% of the time, Pallas kernels for 0%

profile of v1, /device:TPU:2, one launch (start us, length us, event | category | flops | bytes accessed | tf_op | source)
XLA Modules:
  0.0 359.9 jit_solution(3631885361740682616)
XLA Ops:
  7.2 0.0 copy-start
  7.2 0.0 reduce-scatter.2.cloned.1.call-start
  7.2 0.8 bitcast_or_fusion
  8.1 0.8 copy.47
  8.9 0.1 copy.48
  9.0 0.1 reshape.88
  9.1 0.8 copy.51
  9.8 0.1 convert_reduce_fusion.1
  9.9 0.1 reduce_window_sum.11
  10.0 0.0 copy-start.4
  10.0 0.0 copy-start.2
  10.0 0.0 copy-start.3
  10.0 1.9 gather_fusion
  12.0 0.1 reshape.91
  12.1 0.1 copy.49
  12.1 0.0 copy-done.4
  12.2 0.1 copy.50
  12.2 0.4 convert_reduce_fusion
  12.6 0.0 copy-done.2
  12.6 0.5 fusion.10
  13.1 0.0 copy-done.3
  13.1 1.0 fusion.11
  14.1 0.2 pad_maximum_fusion.1
  14.4 63.1 %all_to_all.18 = bf16[64,1,16,1024]{3,2,1,0:T(8,128)(2,1)S(1)} all-to-all(bf16[64,1,16,1024]{3,2,1,0:T(8,128)(2,1)S(1)} %pad_maximum_fusion.1), channel_id=1, replica_groups=mesh['expert'=64,'tensor'=4] {'expert'}, dimensions={0} | all-to-all | bytes 4194304 | tf_op jit(solution)/shard_map/all_to_all | solution.py:40
  77.5 1.1 stack.2
  78.6 96.7 %all_to_all.19 = bf16[4,64,1,16,1024]{4,3,1,2,0:T(8,128)(2,1)} all-to-all(bf16[4,64,1,16,1024]{4,3,1,2,0:T(8,128)(2,1)S(1)} %stack.2), channel_id=1, replica_groups=mesh['expert'=64,'tensor'=4] {'tensor'}, dimensions={0} | all-to-all | bytes 16777216 | tf_op jit(solution)/shard_map/all_to_all | solution.py:42
  175.3 0.0 copy-start.5
  175.3 8.2 %copy.56 = bf16[4,1,64,2,8,1024]{5,4,0,3,2,1:T(8,128)(2,1)} copy(bf16[4,1,64,2,8,1024]{5,4,3,2,1,0:T(8,128)(2,1)} %bitcast.125) | data formatting | bytes 16777216 | tf_op jit(solution)/shard_map/reshape | solution.py:41
  183.5 0.0 copy-done.5
  183.5 4.7 %fusion.18 = f32[64,1,8,384]{3,2,0,1:T(8,128)S(1)} fusion(bf16[1,4096,384]{2,1,0:T(8,128)(2,1)S(1)} %copy-done.5, bf16[64,1,16,4096]{3,2,0,1:T(8,128)(2,1)} %bitcast.127), kind=kOutput, calls=%fused_computation.25 | convolution fusion | flops 1610612736 | bytes 8126464 | tf_op jit(solution)/shard_map/nesd,edh->nesh/dot_general | solution.py:46
  188.1 0.0 copy-done
  188.1 0.0 copy-done.1
  188.2 0.0 copy-start.7
  188.2 2.4 fusion.27
  190.6 0.0 copy-done.7
  190.6 0.0 copy-start.6
  190.6 4.3 %fusion = bf16[64,1,8,4096]{3,2,0,1:T(8,128)(2,1)} fusion(bf16[1,384,4096]{2,1,0:T(8,128)(2,1)S(1)} %copy-done, f32[64,1,8,384]{3,2,0,1:T(8,128)S(1)} %fusion.18), kind=kOutput, calls=%fused_computation.6 | convolution fusion | flops 1613692928 | bytes 8126464 | tf_op jit(solution)/shard_map/nesh,ehd->nesd/dot_general | solution.py:49
  194.9 0.0 copy-done.6
  194.9 4.3 %fusion.1 = bf16[64,1,8,4096]{3,2,0,1:T(8,128)(2,1)} fusion(bf16[64,8,384]{2,1,0:T(8,128)(2,1)S(1)} %fusion.27, bf16[1,4096,384]{2,1,0:T(8,128)(2,1)S(1)} %copy-done.5), kind=kOutput, calls=%fused_computation.7 | convolution fusion | flops 1612709888 | bytes 7733248 | tf_op jit(solution)/shard_map/nesh,edh->nesd/dot_general | solution.py:62
  199.2 7.8 %pad_maximum_fusion = bf16[64,1,16,4096]{3,2,0,1:T(8,128)(2,1)} fusion(bf16[64,1,8,4096]{3,2,0,1:T(8,128)(2,1)} %fusion.1, bf16[64,1,8,4096]{3,2,0,1:T(8,128)(2,1)} %fusion), kind=kLoop, calls=%fused_computation.1 | loop fusion | flops 16777216 | bytes 16777216 | tf_op jit(solution)/shard_map/concatenate | solution.py:63
  207.0 0.0 reduce-scatter.2.cloned.1.call-update
  207.1 6.0 %fusion.3 = bf16[1,384,4096]{2,1,0:T(8,128)(2,1)} fusion(bf16[64,1,16,4096]{3,2,0,1:T(8,128)(2,1)} %bitcast.128, f32[64,1,8,384]{3,2,0,1:T(8,128)} %copy-done.7), kind=kOutput, calls=%fused_computation.9 | convolution fusion | flops 1613168640 | bytes 8126464 | tf_op jit(solution)/shard_map/nesh,nesd->ehd/dot_general | solution.py:56
  213.0 73.0 %reduce-scatter.2.cloned.1.call-done = bf16[64,1,16,1024]{3,2,0,1:T(8,128)(2,1)} async-done(((bf16[64,1,16,4096]{3,2,0,1:T(8,128)(2,1)}), bf16[64,1,16,1024]{3,2,0,1:T(8,128)(2,1)}) %reduce-scatter.2.cloned.1.call-update) | async-done | bytes 2097168 | tf_op jit(solution)/shard_map/reduce_scatter | solution.py:64
  286.0 10.9 %all-to-all-start.2 = ((bf16[64,1,16,1024]{3,2,1,0:T(8,128)(2,1)}), bf16[64,1,16,1024]{3,2,1,0:T(8,128)(2,1)}, u32[]{:S(2)}, u32[]{:S(2)}) async-start(bf16[64,1,16,1024]{3,2,1,0:T(8,128)(2,1)} %bitcast.131), calls=%async_computation.3 | async-start | bytes 4194304 | tf_op jit(solution)/shard_map/all_to_all | solution.py:65
  297.0 6.3 %fusion.2 = bf16[1,4096,384]{2,1,0:T(8,128)(2,1)} fusion(bf16[64,8,384]{2,1,0:T(8,128)(2,1)} %copy-done.6, bf16[64,1,16,4096]{3,2,0,1:T(8,128)(2,1)} %bitcast.129), kind=kOutput, calls=%fused_computation.8 | convolution fusion | flops 1612185600 | bytes 7733248 | tf_op jit(solution)/shard_map/nesd,nesh->edh/dot_general | solution.py:59
  303.3 44.9 %all-to-all-done.2 = bf16[64,1,16,1024]{3,2,1,0:T(8,128)(2,1)} async-done(((bf16[64,1,16,1024]{3,2,1,0:T(8,128)(2,1)}), bf16[64,1,16,1024]{3,2,1,0:T(8,128)(2,1)}, u32[]{:S(2)}, u32[]{:S(2)}) %all-to-all-start.2) | async-done | bytes 2097184 | tf_op jit(solution)/shard_map/all_to_all | solution.py:65
  348.2 2.5 convolution_convert_fusion.4
  350.6 2.5 convolution_convert_fusion.5
  (3 shorter events, 0.0 us)
Async XLA Ops:
  7.2 181.0 %copy-start = (bf16[1,384,4096]{2,1,0:T(8,128)(2,1)S(1)}, bf16[1,384,4096]{2,1,0:T(8,128)(2,1)}, u32[]{:S(2)}) copy-start(bf16[1,384,4096]{2,1,0:T(8,128)(2,1)} %param.11) | copy-start | bytes 9437188
  7.2 278.8 %reduce-scatter.2.cloned.1.call-start = ((), (), s32[]{:S(2)}) async-start(), calls=%async_computation.4 | async-start | bytes 10485760 | tf_op jit(solution)/shard_map/reduce_scatter | solution.py:64
  10.0 2.1 copy-start.4
  10.0 2.6 copy-start.2
  10.0 3.1 copy-start.3
  175.3 8.2 %copy-start.5 = (bf16[1,4096,384]{2,1,0:T(8,128)(2,1)S(1)}, bf16[1,4096,384]{2,1,0:T(8,128)(2,1)}, u32[]{:S(2)}) copy-start(bf16[1,4096,384]{2,1,0:T(8,128)(2,1)} %param.10) | copy-start | bytes 9437188
  183.5 4.7 %copy-start.1 = (bf16[4,1,64,2,8,1024]{5,4,0,3,2,1:T(8,128)(2,1)S(1)}, bf16[4,1,64,2,8,1024]{5,4,0,3,2,1:T(8,128)(2,1)}, u32[]{:S(2)}) copy-start(bf16[4,1,64,2,8,1024]{5,4,0,3,2,1:T(8,128)(2,1)} %copy.56) | copy-start | bytes 25165828
  188.2 2.5 copy-start.7
  190.6 4.3 %copy-start.6 = (bf16[64,8,384]{2,1,0:T(8,128)(2,1)}, bf16[64,8,384]{2,1,0:T(8,128)(2,1)S(1)}, u32[]{:S(2)}) copy-start(bf16[64,8,384]{2,1,0:T(8,128)(2,1)S(1)} %fusion.27) | copy-start | bytes 1179652
  286.0 62.1 %all-to-all-start.2 = ((bf16[64,1,16,1024]{3,2,1,0:T(8,128)(2,1)}), bf16[64,1,16,1024]{3,2,1,0:T(8,128)(2,1)}, u32[]{:S(2)}, u32[]{:S(2)}) async-start(bf16[64,1,16,1024]{3,2,1,0:T(8,128)(2,1)} %bitcast.131), calls=%async_computation.3 | async-start | bytes 4194304 | tf_op jit(solution)/shard_map/all_to_all | solution.py:65
Sparse Core Ops, SparseCore 0:
  207.2 78.7 reduce-scatter.1
